TPU v7x, 32 devices: a whole 2x2x4 slice. The times are simulated.
32 devices in a mesh: member: 2 (over x), row: 16 (over z, y, core).
Axes of the slice: x: 2, y: 2, z: 4, core: 2. Of those that a mesh axis runs over, the one named last changes fastest.
Arguments:
- innovation: bfloat16 [8, 1024, 2048], P('member', 'row'), parts along dimension 0, may hold values from -6 to 6
- background: bfloat16 [8, 1024, 2048], P('member', 'row'), parts along dimension 0, may hold values from -6 to 6
- level_weight: float32 [4], replicated, may hold values from 0.25 to 4
Outputs:
- displacement: float32 [4, 1024, 2048], P('member', 'row'), parts along dimension 0
There are 2 independent parts, one for each index of `member`. A program takes and returns all parts, laid end to end along the dimension named above; an argument that names none is the same for every part. Nothing has to cross between parts.
All inputs are finite; a program needn't handle non-finite values.
Results may differ from a plain program's by a relative error of at most 0.0003.
Values may be sent and summed in bfloat16 or wider, within the bound.
A program may use at most 64 MiB of HBM per device.

v0:
```python
import jax
import jax.numpy as jnp
from jax import lax
from jax.sharding import PartitionSpec as P

HALF = 64
SIGMA = 64


def padded_2(block, sides, width):
    for axis, dim in sides:
        count = lax.axis_size(axis)
        forward = [(i, i + 1) for i in range(count - 1)]
        backward = [(target, source) for source, target in forward]
        low = lax.ppermute(
            lax.slice_in_dim(block, block.shape[dim] - width, None, axis=dim), axis, forward
        )
        high = lax.ppermute(lax.slice_in_dim(block, 0, width, axis=dim), axis, backward)
        block = jnp.concatenate([low, block, high], axis=dim)
    return block


def tap_at(offset):
    grid = jnp.arange(-HALF, HALF + 1).astype(jnp.float32)
    spread = jnp.float32(SIGMA)
    total = jnp.sqrt(jnp.sum(jnp.exp(-grid * grid / (spread * spread))))
    off = offset.astype(jnp.float32)
    value = jnp.exp(-off * off / (2.0 * spread * spread)) / total
    return jnp.where(jnp.abs(offset) <= HALF, value, jnp.float32(0.0))


def band_blocks():
    inner = jnp.arange(128)[:, None]
    outer = jnp.arange(128)[None, :]
    return [tap_at(128 * shift + inner - outer) for shift in (-1, 0, 1)]


def smooth_last(values, blocks):
    lead = values.shape[:-1]
    length = values.shape[-1]
    nblocks = length // 128
    widths = [(0, 0)] * (values.ndim - 1) + [(128, 128)]
    padded = jnp.pad(values, widths).reshape(lead + (nblocks + 2, 128))
    total = jnp.zeros(lead + (nblocks, 128), jnp.float32)
    for index in range(3):
        part = padded[..., index : index + nblocks, :]
        total = total + jnp.dot(
            part, blocks[index], precision=lax.Precision.HIGHEST, preferred_element_type=jnp.float32
        )
    return total.reshape(lead + (length,))


def smooth_mid(values, blocks):
    chans, length, width = values.shape
    nblocks = length // 128
    padded = jnp.pad(values, ((0, 0), (128, 128), (0, 0))).reshape(chans, nblocks + 2, 128, width)
    total = jnp.zeros((chans, nblocks, 128, width), jnp.float32)
    for index in range(3):
        part = padded[:, index : index + nblocks]
        total = total + jnp.einsum(
            "cbix,io->cbox",
            part,
            blocks[index],
            precision=lax.Precision.HIGHEST,
            preferred_element_type=jnp.float32,
        )
    return total.reshape(chans, length, width)


def body(innovation, background, level_weight):
    blocks = band_blocks()
    rimmed = padded_2(background, (("row", 1),), 1).astype(jnp.float32)
    grad_y = 0.5 * (rimmed[:, 2:, :] - rimmed[:, :-2, :])
    padded_x = jnp.pad(rimmed[:, 1:-1, :], ((0, 0), (0, 0), (1, 1)))
    grad_x = 0.5 * (padded_x[:, :, 2:] - padded_x[:, :, :-2])
    scaled = level_weight[:, None, None] * innovation.astype(jnp.float32)
    numer_y = jnp.sum(scaled * grad_y, axis=0)
    numer_x = jnp.sum(scaled * grad_x, axis=0)
    denom = 1.0 + jnp.sum(level_weight[:, None, None] * (grad_y * grad_y + grad_x * grad_x), axis=0)
    raw = jnp.stack([numer_y / denom, numer_x / denom])
    zonal = smooth_last(raw, blocks)
    smoothed = smooth_mid(
        lax.all_to_all(zonal, "row", split_axis=2, concat_axis=1, tiled=True), blocks
    )
    return lax.all_to_all(smoothed, "row", split_axis=1, concat_axis=2, tiled=True)


def solution(mesh):
    placed = (P("member", "row", None), P("member", "row", None), P())
    return jax.shard_map(
        body, mesh=mesh, in_specs=placed, out_specs=P("member", "row", None), check_vma=False
    )
```

profile of v0, /device:TPU:9, one launch (start us, length us, event | category | flops | bytes accessed | tf_op | source)
XLA Modules:
  0.0 94.7 jit_solution(1240667817818672247)
XLA Ops:
  0.0 1.0 %fusion.82 = (bf16[4,1,2048]{2,1,0:T(2,128)(2,1)S(1)}, bf16[4,1,2048]{2,1,0:T(2,128)(2,1)S(1)}) fusion(bf16[4,64,2048]{2,1,0:T(8,128)(2,1)} %param.4), kind=kLoop, calls=%fused_computation.102 | loop fusion | bytes 65536 | tf_op jit(solution)/shard_map/slice | solution.py:16
  1.0 3.7 %collective-permute-start = (bf16[4,1,2048]{2,1,0:T(2,128)(2,1)S(1)}, bf16[4,1,2048]{2,1,0:T(2,128)(2,1)S(1)}, u32[]{:S(2)}, u32[]{:S(2)}) collective-permute-start(bf16[4,1,2048]{2,1,0:T(2,128)(2,1)S(1)} %get-tuple-element.8), channel_id=1, source_target_pairs={{0,1},{1,2},{2,3},{3,4},{4,5},{5,6},{6,7},{7,8},{8,9},{9,10},{10,1... | collective-permute-start | bytes 49160 | tf_op jit(solution)/shard_map/ppermute | solution.py:15
  4.7 1.9 %collective-permute-start.1 = (bf16[4,1,2048]{2,1,0:T(2,128)(2,1)S(1)}, bf16[4,1,2048]{2,1,0:T(2,128)(2,1)S(1)}, u32[]{:S(2)}, u32[]{:S(2)}) collective-permute-start(bf16[4,1,2048]{2,1,0:T(2,128)(2,1)S(1)} %get-tuple-element.9), channel_id=1, source_target_pairs={{1,0},{2,1},{3,2},{4,3},{5,4},{6,5},{7,6},{8,7},{9,8},{10,9},{11,1... | collective-permute-start | bytes 49160 | tf_op jit(solution)/shard_map/ppermute | solution.py:18
  6.7 0.6 fusion.63
  8.0 2.0 %collective-permute-done.1 = bf16[4,1,2048]{2,1,0:T(2,128)(2,1)S(1)} collective-permute-done((bf16[4,1,2048]{2,1,0:T(2,128)(2,1)S(1)}, bf16[4,1,2048]{2,1,0:T(2,128)(2,1)S(1)}, u32[]{:S(2)}, u32[]{:S(2)}) %collective-permute-start.1) | collective-permute-done | bytes 16416 | tf_op jit(solution)/shard_map/ppermute | solution.py:18
  10.0 1.6 %maximum_convert_fusion = f32[4,66,2048]{2,1,0:T(8,128)S(1)} fusion(bf16[4,1,2048]{2,1,0:T(2,128)(2,1)S(1)} %collective-permute-done.1, bf16[4,64,2048]{2,1,0:T(8,128)(2,1)} %param.4, bf16[4,1,2048]{2,1,0:T(2,128)(2,1)S(1)} %collective-permute-done), kind=kLoop, calls=%fused_computation.17 | loop fusion | flops 3244032 | bytes 3244032 | tf_op jit(solution)/shard_map/convert_element_type | solution.py:72
  11.6 0.0 copy-start
  11.6 0.0 copy-start.1
  11.6 0.3 slice.54
  11.9 0.9 copy-done
  12.8 2.7 %multiply_reduce_fusion.2 = (f32[64,2048]{1,0:T(8,128)S(1)}, f32[64,2048]{1,0:T(8,128)S(1)}, f32[64,2048]{1,0:T(8,128)S(1)}) fusion(bf16[4,64,2048]{2,1,0:T(8,128)(2,1)S(1)} %copy-done, f32[4]{0:T(128)S(1)} %copy-done.1, f32[4,66,2048]{2,1,0:T(8,128)S(1)} %maximum_convert_fusion, f32[4,64,2048]{2,1,0:T(8,128)S(1)} %slice.54), kind=kLoop, calls=%fused_computation.8 | loop fusion | flops 8519680 | bytes 8912912 | tf_op jit(solution)/shard_map/reduce_sum | solution.py:77
  15.5 0.1 divide_bitcast_fusion.1
  15.6 0.1 select_maximum_fusion
  15.7 0.2 reshape.52
  15.9 1.0 %fusion.10 = f32[2,64,16,128]{3,2,1,0:T(8,128)S(1)} fusion(f32[2,64,18,128]{3,2,1,0:T(8,128)S(1)} %reshape.52, f32[]{:T(128)S(6)} %sqrt.2, s32[128]{0:T(128)S(1)} %iota_add_fusion.1), kind=kOutput, calls=%fused_computation.25 | convolution fusion | flops 402800640 | bytes 2097668 | tf_op jit(solution)/shard_map/dot_general | solution.py:47
  16.9 1.0 %convolution_add_fusion.3 = f32[2,64,16,128]{3,2,1,0:T(8,128)S(1)} fusion(f32[2,64,16,128]{3,2,1,0:T(8,128)S(1)} %fusion.10, f32[2,64,18,128]{3,2,1,0:T(8,128)S(1)} %reshape.52, f32[]{:T(128)S(6)} %sqrt.2), kind=kOutput, calls=%fused_computation.15 | convolution fusion | flops 403062784 | bytes 3145732 | tf_op jit(solution)/shard_map/dot_general | solution.py:47
  17.9 1.0 %convolution_add_fusion.2 = f32[2,64,16,128]{3,2,1,0:T(8,128)S(1)} fusion(f32[2,64,16,128]{3,2,1,0:T(8,128)S(1)} %convolution_add_fusion.3, f32[2,64,18,128]{3,2,1,0:T(8,128)S(1)} %reshape.52, s32[128]{0:T(128)S(1)} %iota_add_fusion, f32[]{:T(128)S(6)} %sqrt.2), kind=kOutput, calls=%fused_computation.14 | convolution fusion | flops 403062784 | bytes 3146244 | tf_op jit(solution)/shard_map/dot_general | solution.py:47
  18.9 1.0 %copy.30 = f32[2,64,16,128]{1,0,3,2:T(2,128)S(1)} copy(f32[2,64,16,128]{3,2,1,0:T(8,128)S(1)} %convolution_add_fusion.2) | data formatting | bytes 2097152 | tf_op jit(solution)/shard_map/reshape | solution.py:50
  19.9 2.2 %reshape.62 = f32[16,1,16384]{2,1,0:T(1,128)S(1)} reshape(f32[2048,2,64]{2,1,0:T(2,128)S(1)} %bitcast.44) | data formatting | bytes 2097152
  22.1 31.1 %all_to_all.36 = f32[16,1,16384]{2,1,0:T(1,128)S(1)} all-to-all(f32[16,1,16384]{2,1,0:T(1,128)S(1)} %reshape.62), channel_id=1, replica_groups=mesh['member'=2,'row'=16] {'row'}, dimensions={0} | all-to-all | bytes 2097152 | tf_op jit(solution)/shard_map/all_to_all | solution.py:83
  53.2 0.5 broadcast.123
  53.7 3.1 %reduce = f32[16,16384]{1,0:T(8,128)S(1)} reduce(f32[16,1,16384]{2,1,0:T(1,128)S(1)} %all_to_all.36, f32[]{:T(128)} %broadcast.123), dimensions={1}, to_apply=%all_to_all.26.reduce_sub_computation | reduce | bytes 2097156 | tf_op jit(solution)/shard_map/all_to_all | solution.py:83
  56.9 1.5 %reshape.63 = f32[2048,2,64]{2,1,0:T(2,128)S(1)} reshape(f32[16,16384]{1,0:T(8,128)S(1)} %reduce) | data formatting | bytes 2097152
  58.4 0.9 copy.18
  59.3 0.1 pad.14
  59.4 1.1 %fusion.6 = f32[128,2,8,128]{3,0,2,1:T(8,128)S(1)} fusion(f32[2,10,128,128]{3,2,1,0:T(8,128)S(1)} %bitcast.41, f32[]{:T(128)S(6)} %sqrt.2, s32[128]{0:T(128)S(1)} %iota_add_fusion.1), kind=kOutput, calls=%fused_computation.21 | convolution fusion | flops 402800640 | bytes 2097668 | tf_op jit(solution)/shard_map/cbix,io->cbox/dot_general | solution.py:60
  60.5 1.1 %convolution_add_fusion.1 = f32[128,2,8,128]{3,0,2,1:T(8,128)S(1)} fusion(f32[128,2,8,128]{3,0,2,1:T(8,128)S(1)} %fusion.6, f32[2,10,128,128]{3,2,1,0:T(8,128)S(1)} %bitcast.42, f32[]{:T(128)S(6)} %sqrt.2), kind=kOutput, calls=%fused_computation.13 | convolution fusion | flops 403062784 | bytes 3145732 | tf_op jit(solution)/shard_map/cbix,io->cbox/dot_general | solution.py:60
  61.6 1.1 %convolution_add_fusion = f32[128,2,8,128]{3,0,2,1:T(8,128)S(1)} fusion(f32[128,2,8,128]{3,0,2,1:T(8,128)S(1)} %convolution_add_fusion.1, f32[2,10,128,128]{3,2,1,0:T(8,128)S(1)} %bitcast.43, s32[128]{0:T(128)S(1)} %iota_add_fusion, f32[]{:T(128)S(6)} %sqrt.2), kind=kOutput, calls=%fused_computation.12 | convolution fusion | flops 403062784 | bytes 3146244 | tf_op jit(solution)/shard_map/cbix,io->cbox/dot_general | solution.py:60
  62.6 0.8 copy.19
  63.5 29.5 %all_to_all.37 = f32[2,1024,128]{2,0,1:T(2,128)S(1)} all-to-all(f32[2,1024,128]{2,0,1:T(2,128)S(1)} %copy.19), channel_id=1, replica_groups=mesh['member'=2,'row'=16] {'row'}, dimensions={1} | all-to-all | bytes 2097152 | tf_op jit(solution)/shard_map/all_to_all | solution.py:85
  93.0 0.6 copy.20
  93.6 1.1 %all_to_all.33 = f32[2,64,2048]{2,1,0:T(8,128)} reshape(f32[2,64,16,128]{3,2,1,0:T(8,128)S(1)} %copy.20) | data formatting | bytes 2097152 | tf_op jit(solution)/shard_map/all_to_all | solution.py:85
  (4 shorter events, 0.0 us)
Async XLA Ops:
  1.0 7.0 %collective-permute-start = (bf16[4,1,2048]{2,1,0:T(2,128)(2,1)S(1)}, bf16[4,1,2048]{2,1,0:T(2,128)(2,1)S(1)}, u32[]{:S(2)}, u32[]{:S(2)}) collective-permute-start(bf16[4,1,2048]{2,1,0:T(2,128)(2,1)S(1)} %get-tuple-element.8), channel_id=1, source_target_pairs={{0,1},{1,2},{2,3},{3,4},{4,5},{5,6},{6,7},{7,8},{8,9},{9,10},{10,1... | collective-permute-start | bytes 49160 | tf_op jit(solution)/shard_map/ppermute | solution.py:15
  4.7 5.2 %collective-permute-start.1 = (bf16[4,1,2048]{2,1,0:T(2,128)(2,1)S(1)}, bf16[4,1,2048]{2,1,0:T(2,128)(2,1)S(1)}, u32[]{:S(2)}, u32[]{:S(2)}) collective-permute-start(bf16[4,1,2048]{2,1,0:T(2,128)(2,1)S(1)} %get-tuple-element.9), channel_id=1, source_target_pairs={{1,0},{2,1},{3,2},{4,3},{5,4},{6,5},{7,6},{8,7},{9,8},{10,9},{11,1... | collective-permute-start | bytes 49160 | tf_op jit(solution)/shard_map/ppermute | solution.py:18
  11.6 1.2 %copy-start = (bf16[4,64,2048]{2,1,0:T(8,128)(2,1)S(1)}, bf16[4,64,2048]{2,1,0:T(8,128)(2,1)}, u32[]{:S(2)}) copy-start(bf16[4,64,2048]{2,1,0:T(8,128)(2,1)} %param.3) | copy-start | bytes 3145732
  11.6 1.2 %copy-start.1 = (f32[4]{0:T(128)S(1)}, f32[4]{0:T(128)}, u32[]{:S(2)}) copy-start(f32[4]{0:T(128)} %param.5) | copy-start | bytes 52
where the time goes:
time: 95.7 us; the launch traced here: 94.7 us
  blocking collectives  60.6 us (63%)
  local copies, waits for them, and re-layouts  11.2 us (12%)
  other arithmetic  8.24 us (9%)
  matrix products  6.22 us (6%)
  starting transfers between devices  5.63 us (6%)
  waiting for transfers between devices  1.97 us (2%)
    all_to_all x1, blocking collectives, body(): lax.all_to_all(zonal, 'row', split_axis=2, concat_axis=1, tiled=True)  31.1 us
    all_to_all x1, blocking collectives, body(): lax.all_to_all(smoothed, 'row', split_axis=1, concat_axis=2, tiled=True)  29.5 us
    unnamed x6, local copies, waits for them, and re-layouts  4.65 us
    ppermute x1, starting transfers between devices, padded_2(): lax.ppermute(lax.slice_in_dim(block, block.shape[dim] - width, None, axis...  3.71 us
    dot_general x3, matrix products, smooth_mid(): jnp.einsum('cbix,io->cbox', part, blocks[index], precision=lax.Precision....  3.21 us
    all_to_all x1, other arithmetic, body(): lax.all_to_all(zonal, 'row', split_axis=2, concat_axis=1, tiled=True)  3.15 us
    dot_general x3, matrix products, smooth_last(): jnp.dot(part, blocks[index], precision=lax.Precision.HIGHEST, preferred_e...  3.01 us
    reduce_sum x1, other arithmetic, body(): numer_y = jnp.sum(scaled * grad_y, axis=0)  2.69 us
  transfers between devices with their start and end apart: 2, of which 1 were waited for; matrix products, arithmetic and copies ran while one was open for 1% of the time, Pallas kernels for 0%

commit v1 on v0

v1 whole, which is shorter than its diff:
```python
import jax
import jax.numpy as jnp
from jax import lax
from jax.experimental import pallas as pl
from jax.experimental.pallas import tpu as pltpu
from jax.sharding import PartitionSpec as P

HALF = 64
SIGMA = 64
LANES = 128
CHUNK = 512
GROUP = 16
WIDE = 256
SCALE = 4096.0


def tap_at(offset):
    grid = lax.broadcasted_iota(jnp.int32, (8, 2 * LANES), 1) - HALF
    off = grid.astype(jnp.float32)
    spread = jnp.float32(SIGMA)
    squares = jnp.where(grid <= HALF, jnp.exp(-off * off / (spread * spread)), 0.0)
    total = jnp.sqrt(jnp.sum(squares[:1], axis=1, keepdims=True))
    value = offset.astype(jnp.float32)
    value = jnp.exp(-value * value / (2.0 * spread * spread)) / total
    return jnp.where(jnp.abs(offset) <= HALF, value, 0.0)


def halves(value):
    high = value.astype(jnp.bfloat16)
    return high, (value - high.astype(jnp.float32)).astype(jnp.bfloat16)


def encode(raw):
    value = raw * SCALE
    value2 = value * value
    value4 = value2 * value2
    value8 = value4 * value4
    return jnp.where(value < 0.0, -value8, value8).astype(jnp.bfloat16)


def decode(code):
    code = code.astype(jnp.float32)
    size = jnp.exp2(jnp.log2(jnp.abs(code)) * 0.125) * (1.0 / SCALE)
    return jnp.where(code < 0.0, -size, size)


def kernel(
    count, inn_hbm, bg_hbm, lw_ref, out_ref,
    inn, bg, rim, edge_out, edge_in, code_out, code_in, dhigh, dlow,
    mhigh, mlow, whigh, wboth, bhigh, blow,
    in_sem, edge_send, edge_recv, send_sem, recv_sem,
):
    levels, rows, cols = inn.shape
    chunks = cols // CHUNK
    me = lax.axis_index("row")
    has = (me > 0, me < count - 1)
    peer = (jnp.maximum(me - 1, 0), jnp.minimum(me + 1, count - 1))

    load_bg = pltpu.make_async_copy(bg_hbm, bg, in_sem.at[0])
    load_inn = pltpu.make_async_copy(inn_hbm, inn, in_sem.at[1])
    load_bg.start()
    load_inn.start()
    barrier = pltpu.get_barrier_semaphore()
    for side in (0, 1):
        @pl.when(has[side])
        def _():
            pl.semaphore_signal(
                barrier, inc=1, device_id={"row": peer[side]},
                device_id_type=pl.DeviceIdType.MESH,
            )

    zeros = jnp.zeros((levels, rows + 16, LANES), jnp.float32)
    rim[:, :, :LANES] = zeros
    rim[:, :, LANES + cols :] = zeros
    strip = jnp.zeros((2 * rows, LANES), jnp.bfloat16)
    for ref in (mhigh, mlow):
        ref[:, :LANES] = strip
        ref[:, LANES + cols :] = strip

    load_bg.wait()
    for level in range(levels):
        edge_out[0, level : level + 1, :] = bg[level, :16, :].astype(jnp.float32)[:1]
        edge_out[1, level : level + 1, :] = bg[level, rows - 16 :, :].astype(jnp.float32)[15:]
    pl.semaphore_wait(barrier, peer[1] - peer[0])

    def edge_copy(side):
        return pltpu.make_async_remote_copy(
            src_ref=edge_out.at[side], dst_ref=edge_in.at[1 - side],
            send_sem=edge_send.at[side], recv_sem=edge_recv.at[1 - side],
            device_id={"row": peer[side]}, device_id_type=pl.DeviceIdType.MESH,
        )

    def code_copy(side, chunk):
        return pltpu.make_async_remote_copy(
            src_ref=code_out.at[chunk], dst_ref=code_in.at[1 - side, chunk],
            send_sem=send_sem.at[side, chunk], recv_sem=recv_sem.at[1 - side, chunk],
            device_id={"row": peer[side]}, device_id_type=pl.DeviceIdType.MESH,
        )

    for side in (0, 1):
        @pl.when(has[side])
        def _():
            edge_copy(side).start()

    @pl.loop(0, chunks)
    def _(chunk):
        at = pl.multiple_of(chunk * CHUNK, CHUNK)
        for level in range(levels):
            rim[level, 8 : 8 + rows, pl.ds(LANES + at, CHUNK)] = bg[
                level, :, pl.ds(at, CHUNK)
            ].astype(jnp.float32)

    load_inn.wait()

    def raw_tile(group, chunk):
        at = pl.multiple_of(chunk * CHUNK, CHUNK)
        top = 8 + group * GROUP
        wide = CHUNK + 2 * LANES
        numer_y = numer_x = None
        denom = jnp.ones((GROUP, CHUNK), jnp.float32)
        for level in range(levels):
            weight = lw_ref[level]
            line = rim[level, top : top + GROUP, pl.ds(at, wide)]
            left = pltpu.roll(line, 1, 1)[:, LANES : LANES + CHUNK]
            right = pltpu.roll(line, wide - 1, 1)[:, LANES : LANES + CHUNK]
            above = rim[level, top - 1 : top - 1 + GROUP, pl.ds(LANES + at, CHUNK)]
            below = rim[level, top + 1 : top + 1 + GROUP, pl.ds(LANES + at, CHUNK)]
            grad_x = 0.5 * (right - left)
            grad_y = 0.5 * (below - above)
            span = pl.ds(group * GROUP, GROUP)
            scaled = weight * inn[level, span, pl.ds(at, CHUNK)].astype(jnp.float32)
            part_y, part_x = scaled * grad_y, scaled * grad_x
            numer_y = part_y if numer_y is None else numer_y + part_y
            numer_x = part_x if numer_x is None else numer_x + part_x
            denom = denom + weight * (grad_y * grad_y + grad_x * grad_x)
        inverse = 1.0 / denom
        for comp, numer in enumerate((numer_y, numer_x)):
            raw = numer * inverse
            low_row = comp * rows + group * GROUP
            code_out[chunk, low_row : low_row + GROUP, :] = encode(raw)
            high, low = halves(raw)
            base = rows + group * GROUP
            dhigh[comp, base : base + GROUP, pl.ds(at, CHUNK)] = high
            dlow[comp, base : base + GROUP, pl.ds(at, CHUNK)] = low

    groups = rows // GROUP

    @pl.loop(0, chunks)
    def _(chunk):
        for group in range(1, groups - 1):
            raw_tile(group, chunk)

    for side in (0, 1):
        row = 7 if side == 0 else 8 + rows

        @pl.when(has[side])
        def _():
            edge_copy(1 - side).wait_recv()
            for level in range(levels):
                rim[level, row : row + 1, LANES : LANES + cols] = edge_in[
                    side, level : level + 1, :
                ]

        @pl.when(jnp.logical_not(has[side]))
        def _():
            for level in range(levels):
                rim[level, row : row + 1, LANES : LANES + cols] = jnp.zeros(
                    (1, cols), jnp.float32
                )

    for chunk in range(chunks):
        for group in (0, groups - 1):
            raw_tile(group, chunk)
        for side in (0, 1):
            @pl.when(has[side])
            def _():
                code_copy(side, chunk).start()

    inner = lax.broadcasted_iota(jnp.int32, (2 * WIDE, WIDE), 0)
    outer = lax.broadcasted_iota(jnp.int32, (2 * WIDE, WIDE), 1)
    high, low = halves(tap_at(inner - LANES - outer))
    bhigh[...] = high
    blow[...] = low
    outer = lax.broadcasted_iota(jnp.int32, (rows, 3 * rows), 0)
    inner = lax.broadcasted_iota(jnp.int32, (rows, 3 * rows), 1)
    high, low = halves(tap_at(inner - rows - outer))
    whigh[...] = high
    wboth[:rows] = high
    wboth[rows:] = low
    for side in (0, 1):
        base = 2 * rows * side

        @pl.when(jnp.logical_not(has[side]))
        def _():
            blank = jnp.zeros((2, rows, cols), jnp.bfloat16)
            dhigh[:, base : base + rows, :] = blank
            dlow[:, base : base + rows, :] = blank

    def product(a, b):
        return jnp.dot(a, b, preferred_element_type=jnp.float32)

    def zonal(block):
        at = block * WIDE
        high = mhigh[:, at : at + 2 * WIDE]
        low = mlow[:, at : at + 2 * WIDE]
        total = product(high, bhigh[...]) + product(high, blow[...]) + product(low, bhigh[...])
        out_ref[0, :, at : at + WIDE] = total[:rows]
        out_ref[1, :, at : at + WIDE] = total[rows:]

    done = 0
    for chunk in range(chunks):
        at = chunk * CHUNK
        for side in (0, 1):
            base = 2 * rows * side

            @pl.when(has[side])
            def _():
                code_copy(1 - side, chunk).wait_recv()
                for comp in (0, 1):
                    code = code_in[side, chunk, comp * rows : (comp + 1) * rows, :]
                    high, low = halves(decode(code))
                    dhigh[comp, base : base + rows, at : at + CHUNK] = high
                    dlow[comp, base : base + rows, at : at + CHUNK] = low

        for comp in (0, 1):
            both = product(wboth[...], dhigh[comp, :, at : at + CHUNK])
            rest = product(whigh[...], dlow[comp, :, at : at + CHUNK])
            high, low = halves(both[:rows] + (both[rows:] + rest))
            mhigh[comp * rows : (comp + 1) * rows, LANES + at : LANES + at + CHUNK] = high
            mlow[comp * rows : (comp + 1) * rows, LANES + at : LANES + at + CHUNK] = low
        ready = cols // WIDE if chunk == chunks - 1 else ((chunk + 1) * CHUNK - HALF) // WIDE
        for block in range(done, ready):
            zonal(block)
        done = ready

    for side in (0, 1):
        @pl.when(has[side])
        def _():
            edge_copy(side).wait_send()
            for chunk in range(chunks):
                code_copy(side, chunk).wait_send()


def solution(mesh):
    count = mesh.shape["row"]

    def body(innovation, background, level_weight):
        levels, rows, cols = innovation.shape
        assert rows == HALF and cols % CHUNK == 0
        chunks = cols // CHUNK
        f32, bf16 = jnp.float32, jnp.bfloat16

        def call(*args):
            return kernel(count, *args)

        return pl.pallas_call(
            call,
            out_shape=jax.ShapeDtypeStruct((2, rows, cols), f32),
            in_specs=[
                pl.BlockSpec(memory_space=pl.ANY),
                pl.BlockSpec(memory_space=pl.ANY),
                pl.BlockSpec(memory_space=pltpu.SMEM),
            ],
            out_specs=pl.BlockSpec(memory_space=pltpu.VMEM),
            scratch_shapes=[
                pltpu.VMEM((levels, rows, cols), bf16),
                pltpu.VMEM((levels, rows, cols), bf16),
                pltpu.VMEM((levels, rows + 16, cols + 2 * LANES), f32),
                pltpu.VMEM((2, levels, cols), f32),
                pltpu.VMEM((2, levels, cols), f32),
                pltpu.VMEM((chunks, 2 * rows, CHUNK), bf16),
                pltpu.VMEM((2, chunks, 2 * rows, CHUNK), bf16),
                pltpu.VMEM((2, 3 * rows, cols), bf16),
                pltpu.VMEM((2, 3 * rows, cols), bf16),
                pltpu.VMEM((2 * rows, cols + 2 * LANES), bf16),
                pltpu.VMEM((2 * rows, cols + 2 * LANES), bf16),
                pltpu.VMEM((rows, 3 * rows), bf16),
                pltpu.VMEM((2 * rows, 3 * rows), bf16),
                pltpu.VMEM((2 * WIDE, WIDE), bf16),
                pltpu.VMEM((2 * WIDE, WIDE), bf16),
                pltpu.SemaphoreType.DMA((2,)),
                pltpu.SemaphoreType.DMA((2,)),
                pltpu.SemaphoreType.DMA((2,)),
                pltpu.SemaphoreType.DMA((2, chunks)),
                pltpu.SemaphoreType.DMA((2, chunks)),
            ],
            compiler_params=pltpu.CompilerParams(
                collective_id=0, has_side_effects=True, vmem_limit_bytes=40 * 2**20
            ),
            name="align",
        )(innovation, background, level_weight)

    placed = (P("member", "row", None), P("member", "row", None), P())
    return jax.shard_map(
        body, mesh=mesh, in_specs=placed, out_specs=P("member", "row", None), check_vma=False
    )
```

time: 95.7 us -> 23.9 us (0.25)
  blocking collectives: 60.6 us -> 0 us
  Pallas kernels: 0 us -> 19.7 us
  other arithmetic: 8.24 us -> 0 us
  local copies, waits for them, and re-layouts: 11.2 us -> 4.08 us
  matrix products: 6.22 us -> 0 us
  starting transfers between devices: 5.63 us -> 0 us
  waiting for transfers between devices: 1.97 us -> 0 us
    all_to_all x2 -> x0, blocking collectives: 60.6 us -> none  [the longest x1 31.1 us: body(): lax.all_to_all(zonal, 'row', split_axis=2, concat_axis=1, tiled=True)]
    pallas_call x0 -> x1, Pallas kernels: none -> 19.7 us  [body(): pl.pallas_call(call, out_shape=jax.ShapeDtypeStruct((2, rows, cols), f32)...]
    dot_general x6 -> x0, matrix products: 6.22 us -> none  [the longest x3 3.21 us: smooth_mid(): jnp.einsum('cbix,io->cbox', part, blocks[index], precision=lax.Precision....]
    ppermute x2 -> x0, starting transfers between devices: 5.63 us -> none  [the longest x1 3.71 us: padded_2(): lax.ppermute(lax.slice_in_dim(block, block.shape[dim] - width, None, axis...]
    reduce_sum x2 -> x0, other arithmetic: 3.3 us -> none  [the longest x1 2.69 us: body(): numer_y = jnp.sum(scaled * grad_y, axis=0)]
    all_to_all x4 -> x0, local copies, waits for them, and re-layouts: 3.18 us -> none  [the longest x2 1.74 us: body(): lax.all_to_all(smoothed, 'row', split_axis=1, concat_axis=2, tiled=True)]
    all_to_all x1 -> x0, other arithmetic: 3.15 us -> none  [body(): lax.all_to_all(zonal, 'row', split_axis=2, concat_axis=1, tiled=True)]
    reshape x3 -> x0, local copies, waits for them, and re-layouts: 1.99 us -> none  [the longest x1 1.01 us: smooth_last(): return total.reshape(lead + (length,))]
  transfers between devices with their start and end apart: 2 -> 0, of which waited for: 1 -> 0; matrix products, arithmetic and copies ran while one was open for 1% -> 0% of each run, Pallas kernels for 0% -> 0%
where the time goes in v1:
time: 23.9 us; the launch traced here: 23.8 us
  Pallas kernels  19.7 us (82%)
  local copies, waits for them, and re-layouts  4.08 us (17%)
    pallas_call x1, Pallas kernels, body(): pl.pallas_call(call, out_shape=jax.ShapeDtypeStruct((2, rows, cols), f32)...  19.7 us
    unnamed x7, local copies, waits for them, and re-layouts  4.08 us

profile of v1, /device:TPU:9, one launch (start us, length us, event | category | flops | bytes accessed | tf_op | source)
XLA Modules:
  0.0 23.8 jit_solution(17712958706276183015)
XLA Ops:
  0.0 0.0 copy-start
  0.0 1.2 %copy-done = bf16[4,64,2048]{2,1,0:T(8,128)(2,1)S(1)} copy-done((bf16[4,64,2048]{2,1,0:T(8,128)(2,1)S(1)}, bf16[4,64,2048]{2,1,0:T(8,128)(2,1)}, u32[]{:S(2)}) %copy-start) | copy-done | bytes 1048600
  1.2 0.0 copy-start.1
  1.2 1.2 %copy-done.1 = bf16[4,64,2048]{2,1,0:T(8,128)(2,1)S(1)} copy-done((bf16[4,64,2048]{2,1,0:T(8,128)(2,1)S(1)}, bf16[4,64,2048]{2,1,0:T(8,128)(2,1)}, u32[]{:S(2)}) %copy-start.1) | copy-done | bytes 1048600
  2.5 0.0 copy-start.2
  2.5 0.7 %copy-done.2 = f32[4]{0:T(128)S(1)} copy-done((f32[4]{0:T(128)S(1)}, f32[4]{0:T(128)}, u32[]{:S(2)}) %copy-start.2) | copy-done | bytes 40
  3.1 19.7 %align.1 = f32[2,64,2048]{2,1,0:T(8,128)S(1)} custom-call(bf16[4,64,2048]{2,1,0:T(8,128)(2,1)S(1)} %copy-done, bf16[4,64,2048]{2,1,0:T(8,128)(2,1)S(1)} %copy-done.1, f32[4]{0:T(128)S(1)} %copy-done.2), custom_call_target="tpu_custom_call" | custom-call | tf_op jit(solution)/shard_map/align/pallas_call | solution.py:256
  22.8 1.0 %copy.5 = f32[2,64,2048]{2,1,0:T(8,128)} copy(f32[2,64,2048]{2,1,0:T(8,128)S(1)} %align.1) | data formatting | bytes 2097152
Async XLA Ops:
  0.0 1.2 %copy-start = (bf16[4,64,2048]{2,1,0:T(8,128)(2,1)S(1)}, bf16[4,64,2048]{2,1,0:T(8,128)(2,1)}, u32[]{:S(2)}) copy-start(bf16[4,64,2048]{2,1,0:T(8,128)(2,1)} %args_0_.4) | copy-start | bytes 3145732
  1.2 1.2 %copy-start.1 = (bf16[4,64,2048]{2,1,0:T(8,128)(2,1)S(1)}, bf16[4,64,2048]{2,1,0:T(8,128)(2,1)}, u32[]{:S(2)}) copy-start(bf16[4,64,2048]{2,1,0:T(8,128)(2,1)} %args_1_.4) | copy-start | bytes 3145732
  2.5 0.7 %copy-start.2 = (f32[4]{0:T(128)S(1)}, f32[4]{0:T(128)}, u32[]{:S(2)}) copy-start(f32[4]{0:T(128)} %args_2_.4) | copy-start | bytes 52

commit v2 on v1

--- a/solution.py
+++ b/solution.py
@@ -45,13 +45,14 @@
 
 
 def kernel(
-    count, inn_hbm, bg_hbm, lw_ref, out_ref,
-    inn, bg, rim, edge_out, edge_in, code_out, code_in, dhigh, dlow,
+    count, inn_hbm, bg_hbm, lw_hbm, out_ref,
+    lw_ref, inn, bg, rim, edge_out, edge_in, code_out, code_in, dhigh, dlow,
     mhigh, mlow, whigh, wboth, bhigh, blow,
     in_sem, edge_send, edge_recv, send_sem, recv_sem,
 ):
     levels, rows, cols = inn.shape
     chunks = cols // CHUNK
+    phases = ((1, 2), (0, 3))
     me = lax.axis_index("row")
     has = (me > 0, me < count - 1)
     peer = (jnp.maximum(me - 1, 0), jnp.minimum(me + 1, count - 1))
@@ -60,6 +61,8 @@
     load_inn = pltpu.make_async_copy(inn_hbm, inn, in_sem.at[1])
     load_bg.start()
     load_inn.start()
+    load_lw = pltpu.make_async_copy(lw_hbm, lw_ref, in_sem.at[2])
+    load_lw.start()
     barrier = pltpu.get_barrier_semaphore()
     for side in (0, 1):
         @pl.when(has[side])
@@ -90,10 +93,11 @@
             device_id={"row": peer[side]}, device_id_type=pl.DeviceIdType.MESH,
         )
 
-    def code_copy(side, chunk):
+    def code_copy(side, phase, chunk):
         return pltpu.make_async_remote_copy(
-            src_ref=code_out.at[chunk], dst_ref=code_in.at[1 - side, chunk],
-            send_sem=send_sem.at[side, chunk], recv_sem=recv_sem.at[1 - side, chunk],
+            src_ref=code_out.at[phase, chunk], dst_ref=code_in.at[1 - side, phase, chunk],
+            send_sem=send_sem.at[side, phase, chunk],
+            recv_sem=recv_sem.at[1 - side, phase, chunk],
             device_id={"row": peer[side]}, device_id_type=pl.DeviceIdType.MESH,
         )
 
@@ -111,9 +115,10 @@
             ].astype(jnp.float32)
 
     load_inn.wait()
+    load_lw.wait()
 
     def raw_tile(group, chunk):
-        at = pl.multiple_of(chunk * CHUNK, CHUNK)
+        at = chunk * CHUNK
         top = 8 + group * GROUP
         wide = CHUNK + 2 * LANES
         numer_y = numer_x = None
@@ -136,19 +141,24 @@
         inverse = 1.0 / denom
         for comp, numer in enumerate((numer_y, numer_x)):
             raw = numer * inverse
-            low_row = comp * rows + group * GROUP
-            code_out[chunk, low_row : low_row + GROUP, :] = encode(raw)
+            phase = phases.index([pair for pair in phases if group in pair][0])
+            low_row = (2 * comp + phases[phase].index(group)) * GROUP
+            code_out[phase, chunk, low_row : low_row + GROUP, :] = encode(raw)
             high, low = halves(raw)
             base = rows + group * GROUP
             dhigh[comp, base : base + GROUP, pl.ds(at, CHUNK)] = high
             dlow[comp, base : base + GROUP, pl.ds(at, CHUNK)] = low
 
-    groups = rows // GROUP
-
-    @pl.loop(0, chunks)
-    def _(chunk):
-        for group in range(1, groups - 1):
-            raw_tile(group, chunk)
+    def send_phase(phase):
+        for chunk in range(chunks):
+            for group in phases[phase]:
+                raw_tile(group, chunk)
+            for side in (0, 1):
+                @pl.when(has[side])
+                def _():
+                    code_copy(side, phase, chunk).start()
+
+    send_phase(0)
 
     for side in (0, 1):
         row = 7 if side == 0 else 8 + rows
@@ -168,13 +178,7 @@
                     (1, cols), jnp.float32
                 )
 
-    for chunk in range(chunks):
-        for group in (0, groups - 1):
-            raw_tile(group, chunk)
-        for side in (0, 1):
-            @pl.when(has[side])
-            def _():
-                code_copy(side, chunk).start()
+    send_phase(1)
 
     inner = lax.broadcasted_iota(jnp.int32, (2 * WIDE, WIDE), 0)
     outer = lax.broadcasted_iota(jnp.int32, (2 * WIDE, WIDE), 1)
@@ -207,20 +211,27 @@
         out_ref[0, :, at : at + WIDE] = total[:rows]
         out_ref[1, :, at : at + WIDE] = total[rows:]
 
+    def receive(phase, chunk):
+        at = chunk * CHUNK
+        for side in (0, 1):
+            @pl.when(has[side])
+            def _():
+                code_copy(1 - side, phase, chunk).wait_recv()
+                for comp in (0, 1):
+                    for order, group in enumerate(phases[phase]):
+                        low_row = (2 * comp + order) * GROUP
+                        code = code_in[side, phase, chunk, low_row : low_row + GROUP, :]
+                        high, low = halves(decode(code))
+                        base = 2 * rows * side + group * GROUP
+                        dhigh[comp, base : base + GROUP, at : at + CHUNK] = high
+                        dlow[comp, base : base + GROUP, at : at + CHUNK] = low
+
+    for chunk in range(chunks):
+        receive(0, chunk)
     done = 0
     for chunk in range(chunks):
         at = chunk * CHUNK
-        for side in (0, 1):
-            base = 2 * rows * side
-
-            @pl.when(has[side])
-            def _():
-                code_copy(1 - side, chunk).wait_recv()
-                for comp in (0, 1):
-                    code = code_in[side, chunk, comp * rows : (comp + 1) * rows, :]
-                    high, low = halves(decode(code))
-                    dhigh[comp, base : base + rows, at : at + CHUNK] = high
-                    dlow[comp, base : base + rows, at : at + CHUNK] = low
+        receive(1, chunk)
 
         for comp in (0, 1):
             both = product(wboth[...], dhigh[comp, :, at : at + CHUNK])
@@ -237,8 +248,9 @@
         @pl.when(has[side])
         def _():
             edge_copy(side).wait_send()
-            for chunk in range(chunks):
-                code_copy(side, chunk).wait_send()
+            for phase in (0, 1):
+                for chunk in range(chunks):
+                    code_copy(side, phase, chunk).wait_send()
 
 
 def solution(mesh):
@@ -257,19 +269,20 @@
             call,
             out_shape=jax.ShapeDtypeStruct((2, rows, cols), f32),
             in_specs=[
-                pl.BlockSpec(memory_space=pl.ANY),
-                pl.BlockSpec(memory_space=pl.ANY),
-                pl.BlockSpec(memory_space=pltpu.SMEM),
+                pl.BlockSpec(memory_space=pltpu.HBM),
+                pl.BlockSpec(memory_space=pltpu.HBM),
+                pl.BlockSpec(memory_space=pltpu.HBM),
             ],
             out_specs=pl.BlockSpec(memory_space=pltpu.VMEM),
             scratch_shapes=[
+                pltpu.SMEM((levels,), f32),
                 pltpu.VMEM((levels, rows, cols), bf16),
                 pltpu.VMEM((levels, rows, cols), bf16),
                 pltpu.VMEM((levels, rows + 16, cols + 2 * LANES), f32),
                 pltpu.VMEM((2, levels, cols), f32),
                 pltpu.VMEM((2, levels, cols), f32),
-                pltpu.VMEM((chunks, 2 * rows, CHUNK), bf16),
-                pltpu.VMEM((2, chunks, 2 * rows, CHUNK), bf16),
+                pltpu.VMEM((2, chunks, rows, CHUNK), bf16),
+                pltpu.VMEM((2, 2, chunks, rows, CHUNK), bf16),
                 pltpu.VMEM((2, 3 * rows, cols), bf16),
                 pltpu.VMEM((2, 3 * rows, cols), bf16),
                 pltpu.VMEM((2 * rows, cols + 2 * LANES), bf16),
@@ -278,17 +291,17 @@
                 pltpu.VMEM((2 * rows, 3 * rows), bf16),
                 pltpu.VMEM((2 * WIDE, WIDE), bf16),
                 pltpu.VMEM((2 * WIDE, WIDE), bf16),
+                pltpu.SemaphoreType.DMA((3,)),
                 pltpu.SemaphoreType.DMA((2,)),
                 pltpu.SemaphoreType.DMA((2,)),
-                pltpu.SemaphoreType.DMA((2,)),
-                pltpu.SemaphoreType.DMA((2, chunks)),
-                pltpu.SemaphoreType.DMA((2, chunks)),
+                pltpu.SemaphoreType.DMA((2, 2, chunks)),
+                pltpu.SemaphoreType.DMA((2, 2, chunks)),
             ],
             compiler_params=pltpu.CompilerParams(
                 collective_id=0, has_side_effects=True, vmem_limit_bytes=40 * 2**20
             ),
             name="align",
-        )(innovation, background, level_weight)
+        )(*(pltpu.with_memory_space_constraint(v, pltpu.HBM) for v in (innovation, background, level_weight)))
 
     placed = (P("member", "row", None), P("member", "row", None), P())
     return jax.shard_map(

time: 23.9 us -> 18.4 us (0.77)
  local copies, waits for them, and re-layouts: 4.08 us -> 0.97 us
  Pallas kernels: 19.7 us -> 17.3 us
    unnamed x7 -> x1, local copies, waits for them, and re-layouts: 4.08 us -> 0.97 us
    pallas_call x1, Pallas kernels: 19.7 us -> 17.3 us  [body(): pl.pallas_call(call, out_shape=jax.ShapeDtypeStruct((2, rows, cols), f32)...]
where the time goes in v2:
time: 18.4 us; the launch traced here: 18.2 us
  Pallas kernels  17.3 us (94%)
  local copies, waits for them, and re-layouts  0.97 us (5%)
    pallas_call x1, Pallas kernels, body(): pl.pallas_call(call, out_shape=jax.ShapeDtypeStruct((2, rows, cols), f32)...  17.3 us
    unnamed x1, local copies, waits for them, and re-layouts  0.97 us

profile of v2, /device:TPU:9, one launch (start us, length us, event | category | flops | bytes accessed | tf_op | source)
XLA Modules:
  0.0 18.2 jit_solution(15892396767450420637)
XLA Ops:
  0.0 17.3 %align.1 = f32[2,64,2048]{2,1,0:T(8,128)S(1)} custom-call(bf16[4,64,2048]{2,1,0:T(8,128)(2,1)} %args_0_.4, bf16[4,64,2048]{2,1,0:T(8,128)(2,1)} %args_1_.4, f32[4]{0:T(128)} %args_2_.4), custom_call_target="tpu_custom_call" | custom-call | tf_op jit(solution)/shard_map/align/pallas_call | solution.py:268
  17.3 1.0 %copy.5 = f32[2,64,2048]{2,1,0:T(8,128)} copy(f32[2,64,2048]{2,1,0:T(8,128)S(1)} %align.1) | data formatting | bytes 2097152

commit v3 on v2

--- a/solution.py
+++ b/solution.py
@@ -48,7 +48,7 @@
     count, inn_hbm, bg_hbm, lw_hbm, out_ref,
     lw_ref, inn, bg, rim, edge_out, edge_in, code_out, code_in, dhigh, dlow,
     mhigh, mlow, whigh, wboth, bhigh, blow,
-    in_sem, edge_send, edge_recv, send_sem, recv_sem,
+    relay, in_sem, edge_send, edge_recv, send_sem, recv_sem, relay_recv, relay_send,
 ):
     levels, rows, cols = inn.shape
     chunks = cols // CHUNK
@@ -57,6 +57,18 @@
     has = (me > 0, me < count - 1)
     peer = (jnp.maximum(me - 1, 0), jnp.minimum(me + 1, count - 1))
 
+    blocks = count // 4 if count % 4 == 0 else 0
+    pieces = 2 * chunks
+    place = lax.rem(me, 4)
+    where = lax.div(me, 4)
+    if blocks:
+        share = (where * pieces // blocks, (blocks - 1 - where) * pieces // blocks)
+    starts = (place == 0, place == 3)
+    passes = (place == 3, place == 0)
+    partner = jnp.where(place == 0, me + 3, me - 3)
+    corner = starts[0] | starts[1]
+    onward = (me - 4, me + 4)
+
     load_bg = pltpu.make_async_copy(bg_hbm, bg, in_sem.at[0])
     load_inn = pltpu.make_async_copy(inn_hbm, inn, in_sem.at[1])
     load_bg.start()
@@ -72,6 +84,18 @@
                 device_id_type=pl.DeviceIdType.MESH,
             )
 
+    others = (
+        (corner, partner), (corner & (where > 0), onward[0]),
+        (corner & (where < blocks - 1), onward[1]),
+    )
+    for test, other in others if blocks else ():
+        @pl.when(test)
+        def _():
+            pl.semaphore_signal(
+                barrier, inc=1, device_id={"row": other},
+                device_id_type=pl.DeviceIdType.MESH,
+            )
+
     zeros = jnp.zeros((levels, rows + 16, LANES), jnp.float32)
     rim[:, :, :LANES] = zeros
     rim[:, :, LANES + cols :] = zeros
@@ -84,7 +108,10 @@
     for level in range(levels):
         edge_out[0, level : level + 1, :] = bg[level, :16, :].astype(jnp.float32)[:1]
         edge_out[1, level : level + 1, :] = bg[level, rows - 16 :, :].astype(jnp.float32)[15:]
-    pl.semaphore_wait(barrier, peer[1] - peer[0])
+    greeted = peer[1] - peer[0]
+    if blocks:
+        greeted = greeted + sum(jnp.where(test, 1, 0) for test, _ in others)
+    pl.semaphore_wait(barrier, greeted)
 
     def edge_copy(side):
         return pltpu.make_async_remote_copy(
@@ -100,6 +127,46 @@
             recv_sem=recv_sem.at[1 - side, phase, chunk],
             device_id={"row": peer[side]}, device_id_type=pl.DeviceIdType.MESH,
         )
+
+    def relay_copy(side, phase, chunk):
+        piece = phase * chunks + chunk
+        return pltpu.make_async_remote_copy(
+            src_ref=code_out.at[phase, chunk], dst_ref=relay.at[piece],
+            send_sem=send_sem.at[side, phase, chunk], recv_sem=relay_recv.at[piece],
+            device_id={"row": partner}, device_id_type=pl.DeviceIdType.MESH,
+        )
+
+    def onward_copy(side, phase, chunk):
+        piece = phase * chunks + chunk
+        return pltpu.make_async_remote_copy(
+            src_ref=relay.at[piece], dst_ref=code_in.at[1 - side, phase, chunk],
+            send_sem=relay_send.at[piece], recv_sem=recv_sem.at[1 - side, phase, chunk],
+            device_id={"row": onward[side]}, device_id_type=pl.DeviceIdType.MESH,
+        )
+
+    def start_code(side, phase, chunk):
+        if not blocks:
+            @pl.when(has[side])
+            def _():
+                code_copy(side, phase, chunk).start()
+            return
+        indirect = starts[side] & (phase * chunks + chunk < share[side])
+
+        @pl.when(indirect)
+        def _():
+            relay_copy(side, phase, chunk).start()
+
+        @pl.when(has[side] & jnp.logical_not(indirect))
+        def _():
+            code_copy(side, phase, chunk).start()
+
+    def pass_on(phase):
+        for chunk in range(chunks if blocks else 0):
+            for side in (0, 1):
+                @pl.when(passes[side] & (phase * chunks + chunk < share[side]))
+                def _():
+                    relay_copy(side, phase, chunk).wait_recv()
+                    onward_copy(side, phase, chunk).start()
 
     for side in (0, 1):
         @pl.when(has[side])
@@ -154,9 +221,7 @@
             for group in phases[phase]:
                 raw_tile(group, chunk)
             for side in (0, 1):
-                @pl.when(has[side])
-                def _():
-                    code_copy(side, phase, chunk).start()
+                start_code(side, phase, chunk)
 
     send_phase(0)
 
@@ -226,8 +291,10 @@
                         dhigh[comp, base : base + GROUP, at : at + CHUNK] = high
                         dlow[comp, base : base + GROUP, at : at + CHUNK] = low
 
+    pass_on(0)
     for chunk in range(chunks):
         receive(0, chunk)
+    pass_on(1)
     done = 0
     for chunk in range(chunks):
         at = chunk * CHUNK
@@ -251,6 +318,13 @@
             for phase in (0, 1):
                 for chunk in range(chunks):
                     code_copy(side, phase, chunk).wait_send()
+
+    for side in (0, 1):
+        for phase in (0, 1):
+            for chunk in range(chunks if blocks else 0):
+                @pl.when(passes[side] & (phase * chunks + chunk < share[side]))
+                def _():
+                    onward_copy(side, phase, chunk).wait_send()
 
 
 def solution(mesh):
@@ -291,11 +365,14 @@
                 pltpu.VMEM((2 * rows, 3 * rows), bf16),
                 pltpu.VMEM((2 * WIDE, WIDE), bf16),
                 pltpu.VMEM((2 * WIDE, WIDE), bf16),
+                pltpu.VMEM((2 * chunks, rows, CHUNK), bf16),
                 pltpu.SemaphoreType.DMA((3,)),
                 pltpu.SemaphoreType.DMA((2,)),
                 pltpu.SemaphoreType.DMA((2,)),
                 pltpu.SemaphoreType.DMA((2, 2, chunks)),
                 pltpu.SemaphoreType.DMA((2, 2, chunks)),
+                pltpu.SemaphoreType.DMA((2 * chunks,)),
+                pltpu.SemaphoreType.DMA((2 * chunks,)),
             ],
             compiler_params=pltpu.CompilerParams(
                 collective_id=0, has_side_effects=True, vmem_limit_bytes=40 * 2**20

time: 18.4 us -> 19.7 us (1.071)
  the two profiles are of different devices: /device:TPU:9 before, /device:TPU:10 now
where the time goes in v3:
time: 19.7 us; the launch traced here: 19.5 us
  Pallas kernels  18.5 us (94%)
  local copies, waits for them, and re-layouts  0.97 us (5%)
    pallas_call x1, Pallas kernels, body(): pl.pallas_call(call, out_shape=jax.ShapeDtypeStruct((2, rows, cols), f32)...  18.5 us
    unnamed x1, local copies, waits for them, and re-layouts  0.97 us

profile of v3, /device:TPU:10, one launch (start us, length us, event | category | flops | bytes accessed | tf_op | source)
XLA Modules:
  0.0 19.5 jit_solution(4090680881388986419)
XLA Ops:
  0.0 18.5 %align.1 = f32[2,64,2048]{2,1,0:T(8,128)S(1)} custom-call(bf16[4,64,2048]{2,1,0:T(8,128)(2,1)} %args_0_.4, bf16[4,64,2048]{2,1,0:T(8,128)(2,1)} %args_1_.4, f32[4]{0:T(128)} %args_2_.4), custom_call_target="tpu_custom_call" | custom-call | tf_op jit(solution)/shard_map/align/pallas_call | solution.py:342
  18.5 1.0 %copy.5 = f32[2,64,2048]{2,1,0:T(8,128)} copy(f32[2,64,2048]{2,1,0:T(8,128)S(1)} %align.1) | data formatting | bytes 2097152

commit v4 on v3

--- a/solution.py
+++ b/solution.py
@@ -58,11 +58,10 @@
     peer = (jnp.maximum(me - 1, 0), jnp.minimum(me + 1, count - 1))
 
     blocks = count // 4 if count % 4 == 0 else 0
-    pieces = 2 * chunks
     place = lax.rem(me, 4)
     where = lax.div(me, 4)
     if blocks:
-        share = (where * pieces // blocks, (blocks - 1 - where) * pieces // blocks)
+        share = (where * chunks // blocks, (blocks - 1 - where) * chunks // blocks)
     starts = (place == 0, place == 3)
     passes = (place == 3, place == 0)
     partner = jnp.where(place == 0, me + 3, me - 3)
@@ -145,7 +144,7 @@
         )
 
     def start_code(side, phase, chunk):
-        if not blocks:
+        if phase == 1 or not blocks:
             @pl.when(has[side])
             def _():
                 code_copy(side, phase, chunk).start()
@@ -294,7 +293,6 @@
     pass_on(0)
     for chunk in range(chunks):
         receive(0, chunk)
-    pass_on(1)
     done = 0
     for chunk in range(chunks):
         at = chunk * CHUNK
@@ -320,11 +318,10 @@
                     code_copy(side, phase, chunk).wait_send()
 
     for side in (0, 1):
-        for phase in (0, 1):
-            for chunk in range(chunks if blocks else 0):
-                @pl.when(passes[side] & (phase * chunks + chunk < share[side]))
-                def _():
-                    onward_copy(side, phase, chunk).wait_send()
+        for chunk in range(chunks if blocks else 0):
+            @pl.when(passes[side] & (chunk < share[side]))
+            def _():
+                onward_copy(side, 0, chunk).wait_send()
 
 
 def solution(mesh):
@@ -365,14 +362,14 @@
                 pltpu.VMEM((2 * rows, 3 * rows), bf16),
                 pltpu.VMEM((2 * WIDE, WIDE), bf16),
                 pltpu.VMEM((2 * WIDE, WIDE), bf16),
-                pltpu.VMEM((2 * chunks, rows, CHUNK), bf16),
+                pltpu.VMEM((chunks, rows, CHUNK), bf16),
                 pltpu.SemaphoreType.DMA((3,)),
                 pltpu.SemaphoreType.DMA((2,)),
                 pltpu.SemaphoreType.DMA((2,)),
                 pltpu.SemaphoreType.DMA((2, 2, chunks)),
                 pltpu.SemaphoreType.DMA((2, 2, chunks)),
-                pltpu.SemaphoreType.DMA((2 * chunks,)),
-                pltpu.SemaphoreType.DMA((2 * chunks,)),
+                pltpu.SemaphoreType.DMA((chunks,)),
+                pltpu.SemaphoreType.DMA((chunks,)),
             ],
             compiler_params=pltpu.CompilerParams(
                 collective_id=0, has_side_effects=True, vmem_limit_bytes=40 * 2**20

time: 19.7 us -> 19.3 us (0.980)
  the two profiles are of different devices: /device:TPU:10 before, /device:TPU:13 now
where the time goes in v4:
time: 19.3 us; the launch traced here: 19.2 us
  Pallas kernels  18.2 us (94%)
  local copies, waits for them, and re-layouts  0.97 us (5%)
    pallas_call x1, Pallas kernels, body(): pl.pallas_call(call, out_shape=jax.ShapeDtypeStruct((2, rows, cols), f32)...  18.2 us
    unnamed x1, local copies, waits for them, and re-layouts  0.97 us

profile of v4, /device:TPU:13, one launch (start us, length us, event | category | flops | bytes accessed | tf_op | source)
XLA Modules:
  0.0 19.2 jit_solution(1855172642690057149)
XLA Ops:
  0.0 18.2 %align.1 = f32[2,64,2048]{2,1,0:T(8,128)S(1)} custom-call(bf16[4,64,2048]{2,1,0:T(8,128)(2,1)} %args_0_.4, bf16[4,64,2048]{2,1,0:T(8,128)(2,1)} %args_1_.4, f32[4]{0:T(128)} %args_2_.4), custom_call_target="tpu_custom_call" | custom-call | tf_op jit(solution)/shard_map/align/pallas_call | solution.py:339
  18.2 1.0 %copy.5 = f32[2,64,2048]{2,1,0:T(8,128)} copy(f32[2,64,2048]{2,1,0:T(8,128)S(1)} %align.1) | data formatting | bytes 2097152

commit v5 on v2

--- a/solution.py
+++ b/solution.py
@@ -8,7 +8,7 @@
 HALF = 64
 SIGMA = 64
 LANES = 128
-CHUNK = 512
+CHUNK = 256
 GROUP = 16
 WIDE = 256
 SCALE = 4096.0

time: 18.4 us -> 19.7 us (1.071)
  Pallas kernels: 17.3 us -> 18.6 us
    pallas_call x1, Pallas kernels: 17.3 us -> 18.6 us  [body(): pl.pallas_call(call, out_shape=jax.ShapeDtypeStruct((2, rows, cols), f32)...]
where the time goes in v5:
time: 19.7 us; the launch traced here: 19.6 us
  Pallas kernels  18.6 us (94%)
  local copies, waits for them, and re-layouts  0.97 us (5%)
    pallas_call x1, Pallas kernels, body(): pl.pallas_call(call, out_shape=jax.ShapeDtypeStruct((2, rows, cols), f32)...  18.6 us
    unnamed x1, local copies, waits for them, and re-layouts  0.97 us

profile of v5, /device:TPU:9, one launch (start us, length us, event | category | flops | bytes accessed | tf_op | source)
XLA Modules:
  0.0 19.6 jit_solution(4843873837345278473)
XLA Ops:
  0.0 18.6 %align.1 = f32[2,64,2048]{2,1,0:T(8,128)S(1)} custom-call(bf16[4,64,2048]{2,1,0:T(8,128)(2,1)} %args_0_.4, bf16[4,64,2048]{2,1,0:T(8,128)(2,1)} %args_1_.4, f32[4]{0:T(128)} %args_2_.4), custom_call_target="tpu_custom_call" | custom-call | tf_op jit(solution)/shard_map/align/pallas_call | solution.py:268
  18.6 1.0 %copy.5 = f32[2,64,2048]{2,1,0:T(8,128)} copy(f32[2,64,2048]{2,1,0:T(8,128)S(1)} %align.1) | data formatting | bytes 2097152

commit v6 on v5

--- a/solution.py
+++ b/solution.py
@@ -8,7 +8,7 @@
 HALF = 64
 SIGMA = 64
 LANES = 128
-CHUNK = 256
+CHUNK = 1024
 GROUP = 16
 WIDE = 256
 SCALE = 4096.0

time: 19.7 us -> 18.5 us (0.939)
  Pallas kernels: 18.6 us -> 17.4 us
    pallas_call x1, Pallas kernels: 18.6 us -> 17.4 us  [body(): pl.pallas_call(call, out_shape=jax.ShapeDtypeStruct((2, rows, cols), f32)...]
where the time goes in v6:
time: 18.5 us; the launch traced here: 18.3 us
  Pallas kernels  17.4 us (94%)
  local copies, waits for them, and re-layouts  0.97 us (5%)
    pallas_call x1, Pallas kernels, body(): pl.pallas_call(call, out_shape=jax.ShapeDtypeStruct((2, rows, cols), f32)...  17.4 us
    unnamed x1, local copies, waits for them, and re-layouts  0.97 us

profile of v6, /device:TPU:9, one launch (start us, length us, event | category | flops | bytes accessed | tf_op | source)
XLA Modules:
  0.0 18.3 jit_solution(9213778734132275834)
XLA Ops:
  0.0 17.4 %align.1 = f32[2,64,2048]{2,1,0:T(8,128)S(1)} custom-call(bf16[4,64,2048]{2,1,0:T(8,128)(2,1)} %args_0_.4, bf16[4,64,2048]{2,1,0:T(8,128)(2,1)} %args_1_.4, f32[4]{0:T(128)} %args_2_.4), custom_call_target="tpu_custom_call" | custom-call | tf_op jit(solution)/shard_map/align/pallas_call | solution.py:268
  17.4 1.0 %copy.5 = f32[2,64,2048]{2,1,0:T(8,128)} copy(f32[2,64,2048]{2,1,0:T(8,128)S(1)} %align.1) | data formatting | bytes 2097152
